TPU v7x, 32 devices: a whole 2x2x4 slice. The times are simulated.
32 devices in a mesh: narrow: 4 (over y, x), region: 8 (over z, core).
Axes of the slice: x: 2, y: 2, z: 4, core: 2. Of those that a mesh axis runs over, the one named last changes fastest.
Arguments:
- point_feats: bfloat16 [64, 131072], P(None, ('narrow', 'region')), may hold values from -6 to 6
- point_owner: int32 [131072, 1], P(('narrow', 'region')), may hold values from 0 to 31; in each aligned block of 4096 rows (0 to 4095, 4096 to 8191, ...) at most 256 rows name the same one
- point_voxel: int32 [131072], P(('narrow', 'region')), may hold values from 0 to 12287
- weight: bfloat16 [9, 64, 192], replicated, may hold values from -0.15625 to 0.15625
- cotangent: bfloat16 [64, 192, 2048], P(None, 'region', 'narrow'), may hold values from -6 to 6
Outputs:
- conv_out: bfloat16 [64, 192, 2048], P(None, 'region', 'narrow')
- point_grad: bfloat16 [64, 131072], P(None, ('narrow', 'region'))
- weight_grad: float32 [9, 64, 192], replicated
Inputs may be any that keep to these rules, and one draw needn't show every extreme that they name: `point_owner`: among the 4096 points of one device no owner is named more than 256 times, a bound that some block reaches.
All inputs are finite; a program needn't handle non-finite values.
Results may differ from a plain program's by a relative error of at most 0.0036.
Values may be sent and summed in bfloat16 or wider, within the bound.
A program may use at most 192 MiB of HBM per device.

v0:
```python
import math
import jax
import jax.numpy as jnp
from jax import lax
from jax.sharding import PartitionSpec as P

NZ = 64
CY = 8


def extended(cells, sides, width):
    for axis, dim in sides:
        count = lax.axis_size(axis)
        ends = count - 1
        head = lax.slice_in_dim(cells, 0, width, axis=dim)
        tail = lax.slice_in_dim(cells, cells.shape[dim] - width, cells.shape[dim], axis=dim)
        cells = jnp.concatenate(
            [
                lax.ppermute(tail, axis, [(i, (i + 1) % count) for i in range(ends)]),
                cells,
                lax.ppermute(head, axis, [((i + 1) % count, i) for i in range(ends)]),
            ],
            axis=dim,
        )
    return cells


def stack_depth(padded, offsets, depth):
    return jnp.concatenate([padded[..., o : o + depth] for o in offsets], axis=0)


def shards(point_feats, point_owner, point_voxel, weight, cotangent):
    n_narrow = lax.axis_size("narrow")
    n_region = lax.axis_size("region")
    devices = n_narrow * n_region
    chans, points_here = point_feats.shape
    slots = 2 * points_here // devices
    rows_x = cotangent.shape[1]
    voxels = rows_x * CY * NZ
    owner = point_owner[:, 0]
    marks = (owner[:, None] == jnp.arange(devices, dtype=jnp.int32)[None, :]).astype(jnp.int32)
    slot = jnp.sum(jnp.cumsum(marks, axis=0) * marks, axis=1) - 1
    send_feats = jnp.zeros((devices, slots, chans), jnp.bfloat16).at[owner, slot].set(point_feats.T)
    send_feats = send_feats.reshape(devices, slots * chans)
    send_vox = jnp.zeros((devices, slots), jnp.int32).at[owner, slot].set(point_voxel)
    got_feats, got_vox = (
        lax.all_to_all(send_feats, ("narrow", "region"), split_axis=0, concat_axis=0, tiled=True),
        lax.all_to_all(send_vox, ("narrow", "region"), split_axis=0, concat_axis=0, tiled=True),
    )
    incoming = got_feats.reshape(devices * slots, chans).astype(jnp.float32)
    targets = got_vox.reshape(devices * slots)
    sums = jax.ops.segment_sum(incoming, targets, num_segments=voxels)
    grid = sums.T.astype(jnp.bfloat16).reshape(chans, rows_x, CY, NZ)
    grads = cotangent.reshape(chans, rows_x, CY, NZ)
    padded = extended(grid, (("narrow", 2), ("region", 1)), 1)
    gpad = extended(grads, (("narrow", 2), ("region", 1)), 1)
    padded = jnp.pad(padded, ((0, 0), (0, 0), (0, 0), (1, 1)))
    stacked = stack_depth(padded, [0, 1, 2], NZ)
    gpad = jnp.pad(gpad, ((0, 0), (0, 0), (0, 0), (1, 1)))
    gstack = stack_depth(gpad, [2, 1, 0], NZ)
    flipped = weight.reshape(9, chans, 3, chans).transpose(0, 3, 2, 1).reshape(9, chans, 3 * chans)
    result = jnp.zeros((chans, rows_x, CY, NZ), jnp.float32)
    backward = jnp.zeros((chans, rows_x, CY, NZ), jnp.float32)
    kernels = []
    for a in range(3):
        for b in range(3):
            k = a * 3 + b
            window = stacked[:, a : a + rows_x, b : b + CY]
            result = result + jnp.einsum(
                "ok,kxyz->oxyz", weight[k], window, preferred_element_type=jnp.float32
            )
            kernels.append(
                jnp.einsum("oxyz,kxyz->ok", grads, window, preferred_element_type=jnp.float32)
            )
            backward = backward + jnp.einsum(
                "ck,kxyz->cxyz",
                flipped[k],
                gstack[:, 2 - a : 2 - a + rows_x, 2 - b : 2 - b + CY],
                preferred_element_type=jnp.float32,
            )
    conv_out = result.astype(jnp.bfloat16).reshape(chans, rows_x, CY * NZ)
    total_cells = rows_x * n_region * CY * n_narrow * NZ
    weight_grad = lax.psum(jnp.stack(kernels), ("narrow", "region")) * (
        1.0 / math.sqrt(total_cells)
    )
    grad_flat = backward.astype(jnp.bfloat16).reshape(chans, voxels)
    picked = jnp.take(grad_flat, targets, axis=1).T.reshape(devices, slots * chans)
    returned = lax.all_to_all(picked, ("narrow", "region"), split_axis=0, concat_axis=0, tiled=True)
    returned = returned.reshape(devices, slots, chans)
    point_grad = returned[owner, slot].T
    return (conv_out, point_grad, weight_grad)


def solution(mesh):
    in_specs = (
        P(None, ("narrow", "region")),
        P(("narrow", "region"), None),
        P(("narrow", "region")),
        P(),
        P(None, "region", "narrow"),
    )
    out_specs = (P(None, "region", "narrow"), P(None, ("narrow", "region")), P())
    return jax.shard_map(shards, mesh=mesh, in_specs=in_specs, out_specs=out_specs, check_vma=False)
```

profile of v0, /device:TPU:0, one launch (start us, length us, event | category | flops | bytes accessed | tf_op | source)
XLA Modules:
  0.0 687.5 jit_solution(5900122822803206030)
XLA Ops:
  7.9 9.2 %reduce-window.6 = s32[32,32,128]{2,1,0:T(8,128)S(1)} reduce-window(s32[32,32,128]{2,1,0:T(8,128)S(1)} %fusion.21, s32[]{:T(128)} %constant.14.clone.1), window={size=1x1x128 pad=0_0x0_0x127_0}, to_apply=%region_0.0 | reduce-window | flops 16646144 | bytes 1048580 | tf_op jit(solution)/shard_map/reduce-window
  21.8 16.3 %scatter_custom_fusion.1 = s32[8192]{0:T(1024)} fusion(s32[4096]{0:T(1024)S(1)} %broadcast_select_fusion.1, s32[4096]{0:T(1024)} %param.7, s32[]{:T(128)} %constant.14.clone.1), kind=kCustom, calls=%fused_computation.98 | custom fusion | bytes 33280
  38.1 7.4 %all-to-all-start = ((s32[32,1,256]{2,1,0:T(1,128)}), s32[32,1,256]{2,1,0:T(1,128)}, u32[]{:S(2)}, u32[]{:S(2)}) async-start(s32[32,1,256]{2,1,0:T(1,128)} %bitcast.5), calls=%async_computation | async-start | bytes 65536 | tf_op jit(solution)/shard_map/all_to_all | solution.py:48
  45.5 3.4 copy.56
  49.9 3.6 collective-permute-start.4
  58.5 2.4 copy.54
  60.9 12.9 %scatter_custom_fusion.2 = bf16[8192,64]{1,0:T(8,128)(2,1)} fusion(s32[4096]{0:T(1024)} %copy-done.17, bf16[4096,64]{1,0:T(8,128)(2,1)} %copy.54, bf16[]{:T(256)} %constant.33.clone.1), kind=kCustom, calls=%fused_computation.45 | custom fusion | bytes 1049088
  73.8 6.2 all_to_all.24
  80.6 9.4 %reduce.11 = bf16[32,16384]{1,0:T(8,128)(2,1)} reduce(bf16[32,1,16384]{2,1,0:T(2,128)(2,1)} %all_to_all.24, bf16[]{:T(256)} %broadcast.231), dimensions={1}, to_apply=%all_to_all.24.reduce_sub_computation | reduce | bytes 2097154 | tf_op jit(solution)/shard_map/all_to_all | solution.py:47
  89.9 2.6 reshape.224
  106.1 7.6 %all-to-all-start.1 = ((bf16[32,2,8192]{2,1,0:T(2,128)(2,1)}), bf16[32,2,8192]{2,1,0:T(2,128)(2,1)}, u32[]{:S(2)}, u32[]{:S(2)}) async-start(bf16[32,2,8192]{2,1,0:T(2,128)(2,1)} %reshape.224), calls=%async_computation.1 | async-start | bytes 2097152 | tf_op jit(solution)/shard_map/all_to_all | solution.py:47
  122.4 9.0 %select_maximum_fusion = bf16[64,26,10,66]{0,3,2,1:T(8,128)(2,1)S(1)} fusion(bf16[64,1,10,64]{0,3,2,1:T(8,128)(2,1)S(1)} %collective-permute-done.7, bf16[64,1,10,64]{0,3,2,1:T(8,128)(2,1)S(1)} %collective-permute-done.6, bf16[64,24,1,64]{0,3,2,1:T(8,128)(2,1)} %collective-permute-done.5, bf16[64,24,8,64]{0,3,2,1:T(8,128)(2,1)S(1)} %bitcast.265, ...), kind=kLoop, calls=%fused_computation.12 | loop fusion | flops 19768320 | bytes 4326400 | tf_op jit(solution)/shard_map/concatenate | solution.py:17
  131.4 2.4 fusion.50
  133.8 11.6 %pad_maximum_fusion.1 = bf16[192,26,10,64]{0,3,2,1:T(8,128)(2,1)S(1)} fusion(bf16[64,26,10,64]{0,3,2,1:T(8,128)(2,1)S(1)} %get-tuple-element.15, bf16[64,1,10,64]{0,3,2,1:T(8,128)(2,1)S(1)} %collective-permute-done.7, bf16[64,24,1,64]{0,3,2,1:T(8,128)(2,1)} %collective-permute-done.5, bf16[64,24,8,64]{0,3,2,1:T(8,128)(2,1)S(1)} %bitcast.266, ...), kind=kLoop, calls=%fused_computation.9 | loop fusion | flops 44728320 | bytes 12779520 | tf_op jit(solution)/shard_map/concatenate | solution.py:29
  145.4 4.4 fusion.55
  149.8 4.4 fusion.56
  154.3 4.4 fusion.57
  158.7 4.4 fusion.58
  163.0 4.5 fusion.59
  167.5 4.4 fusion.60
  171.9 4.4 fusion.61
  176.3 4.9 fusion.62
  181.2 18.4 %add_convert_fusion = bf16[24,8,64,64]{3,2,1,0:T(8,128)(2,1)} fusion(f32[24,8,64,64]{3,2,1,0:T(8,128)} %fusion.62, f32[24,8,64,64]{3,2,1,0:T(8,128)} %fusion.61, f32[24,8,64,64]{3,2,1,0:T(8,128)} %fusion.60, f32[24,8,64,64]{3,2,1,0:T(8,128)} %fusion.59, f32[24,8,64,64]{3,2,1,0:T(8,128)} %fusion.58, f32[24,8,64,64]{3,2,1,0:T(8,128)} %fusion.57, ...), kind=kOutput, calls=%fused_computation.10 | convolution fusion | flops 309067776 | bytes 33153024 | tf_op jit(solution)/shard_map/ck,kxyz->cxyz/dot_general | solution.py:75
  199.6 30.4 %gather_fusion = bf16[8192,64]{1,0:T(8,128)(2,1)} fusion(bf16[64,12288]{0,1:T(8,128)(2,1)} %bitcast.281, s32[8192]{0:T(1024)S(1)} %copy-done.15), kind=kCustom, calls=%fused_computation | custom fusion | bytes 2129920 | tf_op jit(solution)/shard_map/jit(_take)/gather | solution.py:87
  230.1 6.6 broadcast_select_fusion
  236.6 6.2 all_to_all.25
  242.8 9.4 %reduce.12 = bf16[32,16384]{1,0:T(8,128)(2,1)} reduce(bf16[32,1,16384]{2,1,0:T(2,128)(2,1)} %all_to_all.25, bf16[]{:T(256)} %broadcast.231), dimensions={1}, to_apply=%all_to_all.25.reduce_sub_computation | reduce | bytes 2097154 | tf_op jit(solution)/shard_map/all_to_all | solution.py:88
  252.2 2.6 reshape.226
  254.8 21.9 %all-to-all-start.2 = ((bf16[32,2,8192]{2,1,0:T(2,128)(2,1)}), bf16[32,2,8192]{2,1,0:T(2,128)(2,1)}, u32[]{:S(2)}, u32[]{:S(2)}) async-start(bf16[32,2,8192]{2,1,0:T(2,128)(2,1)} %reshape.226), calls=%async_computation.2 | async-start | bytes 2097152 | tf_op jit(solution)/shard_map/all_to_all | solution.py:88
  276.8 5.9 reshape.225
  282.7 9.0 %convert_reduce_fusion = f32[32,16384]{1,0:T(8,128)} fusion(bf16[32,1,16384]{2,1,0:T(2,128)(2,1)} %reshape.225), kind=kLoop, calls=%fused_computation.25 | loop fusion | flops 524288 | bytes 3145728 | tf_op jit(solution)/shard_map/convert_element_type | solution.py:50
  291.7 4.3 reshape.171
  296.0 52.3 %scatter_custom_fusion = f32[12288,64]{1,0:T(8,128)} fusion(s32[8192]{0:T(1024)} %bitcast.6, f32[8192,64]{1,0:T(8,128)} %reshape.171, f32[]{:T(128)} %constant.13.clone.1), kind=kCustom, calls=%fused_computation.23 | custom fusion | flops 524288 | bytes 3146240 | tf_op jit(solution)/shard_map/scatter-add | solution.py:52
  348.3 3.0 convert_element_type.29
  351.4 8.3 %collective-permute-start = (bf16[64,24,1,64]{0,3,2,1:T(8,128)(2,1)S(1)}, bf16[64,24,1,64]{0,3,2,1:T(8,128)(2,1)S(1)}, u32[]{:S(2)}, u32[]{:S(2)}) collective-permute-start(bf16[64,24,1,64]{0,3,2,1:T(8,128)(2,1)S(1)} %get-tuple-element.24), channel_id=1, source_target_pairs={{0,8},{8,16},{16,24},{1,9},{9,17},{17,25},{2,10},{10,18},{18,26},{... | collective-permute-start | bytes 589832 | tf_op jit(solution)/shard_map/ppermute | solution.py:19
  361.1 4.0 collective-permute-done
  365.0 5.9 collective-permute-done.1
  375.1 6.2 reshape.227
  381.3 8.7 %reduce.6 = bf16[32,16384]{1,0:T(8,128)(2,1)} reduce(bf16[32,1,16384]{2,1,0:T(2,128)(2,1)} %reshape.227, bf16[]{:T(256)} %constant.72), dimensions={1}, to_apply=%all_to_all.23.reduce_sub_computation | reduce | bytes 2097154 | tf_op jit(solution)/shard_map/all_to_all | solution.py:88
  390.0 4.0 reshape.141
  394.0 67.6 %gather_fusion.1 = bf16[4096,64]{1,0:T(8,128)(2,1)} fusion(bf16[32,256,64]{2,1,0:T(8,128)(2,1)} %reshape.141, s32[4096]{0:T(1024)S(1)} %bitcast.276), kind=kCustom, calls=%fused_computation.1 | custom fusion | bytes 1081344 | tf_op jit(solution)/shard_map/gather | solution.py:90
  461.6 2.3 copy.87
  464.0 9.6 %select_maximum_fusion.4 = bf16[64,26,10,66]{0,3,2,1:T(8,128)(2,1)S(1)} fusion(bf16[64,1,10,64]{0,3,2,1:T(8,128)(2,1)} %collective-permute-done.3, bf16[64,1,10,64]{0,3,2,1:T(8,128)(2,1)} %collective-permute-done.2, bf16[64,24,1,64]{0,3,2,1:T(8,128)(2,1)} %copy-done.3, bf16[64,24,8,64]{0,3,2,1:T(8,128)(2,1)} %bitcast.279, ...), kind=kLoop, calls=%fused_computation.16 | loop fusion | flops 19768320 | bytes 4326400 | tf_op jit(solution)/shard_map/concatenate | solution.py:17
  473.6 2.3 fusion.51
  475.9 11.3 %pad_maximum_fusion = bf16[192,26,10,64]{0,3,2,1:T(8,128)(2,1)S(1)} fusion(bf16[64,26,10,64]{0,3,2,1:T(8,128)(2,1)S(1)} %get-tuple-element.17, bf16[64,1,10,64]{0,3,2,1:T(8,128)(2,1)} %collective-permute-done.3, bf16[64,24,1,64]{0,3,2,1:T(8,128)(2,1)S(1)} %copy-done.4, bf16[64,24,8,64]{0,3,2,1:T(8,128)(2,1)S(1)} %bitcast.280, ...), kind=kLoop, calls=%fused_computation.8 | loop fusion | flops 44728320 | bytes 12779520 | tf_op jit(solution)/shard_map/concatenate | solution.py:29
  487.2 2.8 fusion.16
  490.0 4.5 fusion.23
  494.4 4.3 fusion.25
  498.8 4.4 fusion.27
  503.2 4.4 fusion.29
  507.6 4.4 fusion.31
  512.0 4.3 fusion.33
  516.3 4.4 fusion.35
  520.7 4.6 fusion.37
  527.4 2.1 fusion.14
  529.5 2.1 fusion.13
  531.7 2.1 fusion.12
  533.8 2.1 fusion.11
  535.9 2.1 fusion.10
  538.0 2.1 fusion.9
  540.2 2.1 fusion.8
  542.3 18.5 %add_convert_fusion.1 = bf16[24,8,64,64]{3,2,1,0:T(8,128)(2,1)S(1)} fusion(f32[24,8,64,64]{3,2,1,0:T(8,128)} %fusion.23, f32[24,8,64,64]{3,2,1,0:T(8,128)} %fusion.25, f32[24,8,64,64]{3,2,1,0:T(8,128)} %fusion.27, f32[24,8,64,64]{3,2,1,0:T(8,128)} %fusion.29, f32[24,8,64,64]{3,2,1,0:T(8,128)} %fusion.31, f32[24,8,64,64]{3,2,1,0:T(8,128)} %fusion.33, ...), kind=kOutput, calls=%fused_computation.11 | convolution fusion | flops 309067776 | bytes 33161216 | tf_op jit(solution)/shard_map/ok,kxyz->oxyz/dot_general | solution.py:69
  560.8 3.1 copy.86
  564.0 114.5 %all-reduce.4.cloned.1.call-done = f32[9,64,192]{2,1,0:T(8,128)} async-done(((f32[9,64,192]{2,1,0:T(8,128)}), f32[9,64,192]{2,1,0:T(8,128)}) %all-reduce.4.cloned.1.call-update) | async-done | bytes 442384 | tf_op jit(solution)/shard_map/psum | solution.py:83
  (84 shorter events, 43.8 us)
Async XLA Ops:
  21.8 16.3 %copy-start.17 = (s32[4096]{0:T(1024)}, s32[4096]{0:T(1024)S(1)}, u32[]{:S(2)}) copy-start(s32[4096]{0:T(1024)S(1)} %broadcast_select_fusion.1) | copy-start | bytes 49156
  38.1 68.0 %all-to-all-start = ((s32[32,1,256]{2,1,0:T(1,128)}), s32[32,1,256]{2,1,0:T(1,128)}, u32[]{:S(2)}, u32[]{:S(2)}) async-start(s32[32,1,256]{2,1,0:T(1,128)} %bitcast.5), calls=%async_computation | async-start | bytes 65536 | tf_op jit(solution)/shard_map/all_to_all | solution.py:48
  49.9 65.2 %collective-permute-start.4 = (bf16[64,24,1,64]{0,3,2,1:T(8,128)(2,1)}, bf16[64,24,1,64]{0,3,2,1:T(8,128)(2,1)S(1)}, u32[]{:S(2)}, u32[]{:S(2)}) collective-permute-start(bf16[64,24,1,64]{0,3,2,1:T(8,128)(2,1)} %get-tuple-element.22), channel_id=1, source_target_pairs={{0,8},{8,16},{16,24},{1,9},{9,17},{17,25},{2,10},{10,18},{18,26},{... | collective-permute-start | bytes 589832 | tf_op jit(solution)/shard_map/ppermute | solution.py:19
  53.5 61.6 %collective-permute-start.5 = (bf16[64,24,1,64]{0,3,2,1:T(8,128)(2,1)}, bf16[64,24,1,64]{0,3,2,1:T(8,128)(2,1)}, u32[]{:S(2)}, u32[]{:S(2)}) collective-permute-start(bf16[64,24,1,64]{0,3,2,1:T(8,128)(2,1)} %get-tuple-element.23), channel_id=1, source_target_pairs={{8,0},{16,8},{24,16},{9,1},{17,9},{25,17},{10,2},{18,10},{26,18},{... | collective-permute-start | bytes 589832 | tf_op jit(solution)/shard_map/ppermute | solution.py:21
  106.1 148.8 %all-to-all-start.1 = ((bf16[32,2,8192]{2,1,0:T(2,128)(2,1)}), bf16[32,2,8192]{2,1,0:T(2,128)(2,1)}, u32[]{:S(2)}, u32[]{:S(2)}) async-start(bf16[32,2,8192]{2,1,0:T(2,128)(2,1)} %reshape.224), calls=%async_computation.1 | async-start | bytes 2097152 | tf_op jit(solution)/shard_map/all_to_all | solution.py:47
  115.9 4.8 collective-permute-start.6
  118.0 4.4 collective-permute-start.7
  133.7 11.6 %copy-start.7 = (bf16[1,64,3,64]{1,3,2,0:T(8,128)(2,1)S(1)}, bf16[1,64,3,64]{1,3,2,0:T(8,128)(2,1)}, u32[]{:S(2)}) copy-start(bf16[1,64,3,64]{1,3,2,0:T(8,128)(2,1)} %copy.58) | copy-start | bytes 73732
  145.4 4.5 copy-start.8
  149.8 4.4 copy-start.9
  154.3 4.4 copy-start.10
  158.6 4.4 copy-start.11
  163.0 4.5 copy-start.12
  167.5 4.4 copy-start.13
  171.9 4.4 copy-start.14
  176.3 4.9 copy-start.6
  181.2 18.4 %copy-start.15 = (s32[8192]{0:T(1024)S(1)}, s32[8192]{0:T(1024)}, u32[]{:S(2)}) copy-start(s32[8192]{0:T(1024)} %broadcast_clamp_fusion) | copy-start | bytes 98308
  199.6 30.4 %copy-start.16 = (pred[8192]{0:T(1024)(128)(4,1)S(1)}, pred[8192]{0:T(1024)(128)(4,1)}, u32[]{:S(2)}) copy-start(pred[8192]{0:T(1024)(128)(4,1)} %compare_and_fusion) | copy-start | bytes 24580
  254.8 120.2 %all-to-all-start.2 = ((bf16[32,2,8192]{2,1,0:T(2,128)(2,1)}), bf16[32,2,8192]{2,1,0:T(2,128)(2,1)}, u32[]{:S(2)}, u32[]{:S(2)}) async-start(bf16[32,2,8192]{2,1,0:T(2,128)(2,1)} %reshape.226), calls=%async_computation.2 | async-start | bytes 2097152 | tf_op jit(solution)/shard_map/all_to_all | solution.py:88
  276.8 401.7 %all-reduce.4.cloned.1.call-start = ((), (), s32[]{:S(2)}) async-start(), calls=%async_computation.3 | async-start | bytes 1179648 | tf_op jit(solution)/shard_map/psum | solution.py:83
  351.4 19.6 %copy-start.1 = (bf16[12288,64]{1,0:T(8,128)(2,1)}, bf16[12288,64]{1,0:T(8,128)(2,1)S(1)}, u32[]{:S(2)}) copy-start(bf16[12288,64]{1,0:T(8,128)(2,1)S(1)} %convert_element_type.29) | copy-start | bytes 4718596
  351.4 13.6 %collective-permute-start = (bf16[64,24,1,64]{0,3,2,1:T(8,128)(2,1)S(1)}, bf16[64,24,1,64]{0,3,2,1:T(8,128)(2,1)S(1)}, u32[]{:S(2)}, u32[]{:S(2)}) collective-permute-start(bf16[64,24,1,64]{0,3,2,1:T(8,128)(2,1)S(1)} %get-tuple-element.24), channel_id=1, source_target_pairs={{0,8},{8,16},{16,24},{1,9},{9,17},{17,25},{2,10},{10,18},{18,26},{... | collective-permute-start | bytes 589832 | tf_op jit(solution)/shard_map/ppermute | solution.py:19
  359.8 11.2 %collective-permute-start.1 = (bf16[64,24,1,64]{0,3,2,1:T(8,128)(2,1)S(1)}, bf16[64,24,1,64]{0,3,2,1:T(8,128)(2,1)S(1)}, u32[]{:S(2)}, u32[]{:S(2)}) collective-permute-start(bf16[64,24,1,64]{0,3,2,1:T(8,128)(2,1)S(1)} %get-tuple-element.25), channel_id=1, source_target_pairs={{8,0},{16,8},{24,16},{9,1},{17,9},{25,17},{10,2},{18,10},{26,18},{... | collective-permute-start | bytes 589832 | tf_op jit(solution)/shard_map/ppermute | solution.py:21
  370.9 0.9 copy-start.3
  371.8 92.2 %collective-permute-start.2 = (bf16[64,1,10,64]{0,3,2,1:T(8,128)(2,1)}, bf16[64,1,10,64]{0,3,2,1:T(8,128)(2,1)}, u32[]{:S(2)}, u32[]{:S(2)}) collective-permute-start(bf16[64,1,10,64]{0,3,2,1:T(8,128)(2,1)} %get-tuple-element.20), channel_id=1, source_target_pairs={{0,1},{1,2},{2,3},{3,4},{4,5},{5,6},{6,7},{8,9},{9,10},{10,11},{11... | collective-permute-start | bytes 245768 | tf_op jit(solution)/shard_map/ppermute | solution.py:19
  373.8 90.2 %collective-permute-start.3 = (bf16[64,1,10,64]{0,3,2,1:T(8,128)(2,1)}, bf16[64,1,10,64]{0,3,2,1:T(8,128)(2,1)}, u32[]{:S(2)}, u32[]{:S(2)}) collective-permute-start(bf16[64,1,10,64]{0,3,2,1:T(8,128)(2,1)} %get-tuple-element.21), channel_id=1, source_target_pairs={{1,0},{2,1},{3,2},{4,3},{5,4},{6,5},{7,6},{9,8},{10,9},{11,10},{12... | collective-permute-start | bytes 245768 | tf_op jit(solution)/shard_map/ppermute | solution.py:21
  473.5 2.4 copy-start.2
  473.6 2.4 copy-start.4
  487.2 53.0 %copy-start = (bf16[192,26,10,64]{0,3,2,1:T(8,128)(2,1)}, bf16[192,26,10,64]{0,3,2,1:T(8,128)(2,1)S(1)}, u32[]{:S(2)}) copy-start(bf16[192,26,10,64]{0,3,2,1:T(8,128)(2,1)S(1)} %pad_maximum_fusion) | copy-start | bytes 19169284
  487.2 2.8 copy-start.5
Sparse Core Ops, SparseCore 0:
  542.4 135.9 all-reduce.3
where the time goes:
time: 696 us; the launch traced here: 687 us
  local copies, waits for them, and re-layouts  201 us (29%)
  other arithmetic  160 us (23%)
  matrix products  128 us (18%)
  waiting for transfers between devices  126 us (18%)
  starting transfers between devices  58.1 us (8%)
  between operations  14.6 us (2%)
    psum x1, waiting for transfers between devices, shards(): lax.psum(jnp.stack(kernels), ('narrow', 'region'))  114 us
    gather x1, local copies, waits for them, and re-layouts, shards(): point_grad = returned[owner, slot].T  67.6 us
    unnamed x46, local copies, waits for them, and re-layouts  57.5 us
    dot_general x9, matrix products, shards(): jnp.einsum('ck,kxyz->cxyz', flipped[k], gstack[:, 2 - a:2 - a + rows_x, 2...  54.2 us
    dot_general x9, matrix products, shards(): jnp.einsum('ok,kxyz->oxyz', weight[k], window, preferred_element_type=jnp...  53.8 us
    scatter-add x1, other arithmetic, shards(): sums = jax.ops.segment_sum(incoming, targets, num_segments=voxels)  52.3 us
    gather x1, local copies, waits for them, and re-layouts, shards(): jnp.take(grad_flat, targets, axis=1).T.reshape(devices, slots * chans)  30.4 us
    concatenate x2, other arithmetic, stack_depth(): return jnp.concatenate([padded[..., o:o + depth] for o in offsets], axis=0)  22.9 us
  transfers between devices with their start and end apart: 12, of which 4 were waited for; matrix products, arithmetic and copies ran while one was open for 53% of the time, Pallas kernels for 0%

commit v1 on v0

--- a/solution.py
+++ b/solution.py
@@ -80,7 +80,7 @@
             )
     conv_out = result.astype(jnp.bfloat16).reshape(chans, rows_x, CY * NZ)
     total_cells = rows_x * n_region * CY * n_narrow * NZ
-    weight_grad = lax.psum(jnp.stack(kernels), ("narrow", "region")) * (
+    weight_grad = lax.psum(lax.psum(jnp.stack(kernels), "region"), "narrow") * (
         1.0 / math.sqrt(total_cells)
     )
     grad_flat = backward.astype(jnp.bfloat16).reshape(chans, voxels)

time: 696 us -> 669 us (0.961)
  waiting for transfers between devices: 126 us -> 96.2 us
    psum x1 -> x2, waiting for transfers between devices: 114 us -> 84.6 us  [the longest x1 58.3 us: shards(): lax.psum(jnp.stack(kernels), 'region')]
  transfers between devices with their start and end apart: 12 -> 13, of which waited for: 4 -> 5; matrix products, arithmetic and copies ran while one was open for 53% -> 56% of each run, Pallas kernels for 0% -> 0%
where the time goes in v1:
time: 669 us; the launch traced here: 661 us
  local copies, waits for them, and re-layouts  201 us (30%)
  other arithmetic  160 us (24%)
  matrix products  131 us (20%)
  waiting for transfers between devices  96.2 us (14%)
  starting transfers between devices  58.2 us (9%)
  between operations  14.6 us (2%)
    gather x1, local copies, waits for them, and re-layouts, shards(): point_grad = returned[owner, slot].T  67.6 us
    psum x1, waiting for transfers between devices, shards(): lax.psum(jnp.stack(kernels), 'region')  58.3 us
    unnamed x46, local copies, waits for them, and re-layouts  57.5 us
    dot_general x9, matrix products, shards(): jnp.einsum('ok,kxyz->oxyz', weight[k], window, preferred_element_type=jnp...  56.6 us
    dot_general x9, matrix products, shards(): jnp.einsum('ck,kxyz->cxyz', flipped[k], gstack[:, 2 - a:2 - a + rows_x, 2...  54.2 us
    scatter-add x1, other arithmetic, shards(): sums = jax.ops.segment_sum(incoming, targets, num_segments=voxels)  52.3 us
    gather x1, local copies, waits for them, and re-layouts, shards(): jnp.take(grad_flat, targets, axis=1).T.reshape(devices, slots * chans)  30.4 us
    psum x1, waiting for transfers between devices, shards(): lax.psum(lax.psum(jnp.stack(kernels), 'region'), 'narrow')  26.2 us
  transfers between devices with their start and end apart: 13, of which 5 were waited for; matrix products, arithmetic and copies ran while one was open for 56% of the time, Pallas kernels for 0%

profile of v1, /device:TPU:0, one launch (start us, length us, event | category | flops | bytes accessed | tf_op | source)
XLA Modules:
  0.0 660.6 jit_solution(17439571040194345483)
XLA Ops:
  7.9 9.2 %reduce-window.6 = s32[32,32,128]{2,1,0:T(8,128)S(1)} reduce-window(s32[32,32,128]{2,1,0:T(8,128)S(1)} %fusion.21, s32[]{:T(128)} %constant.14.clone.1), window={size=1x1x128 pad=0_0x0_0x127_0}, to_apply=%region_0.0 | reduce-window | flops 16646144 | bytes 1048580 | tf_op jit(solution)/shard_map/reduce-window
  21.8 16.3 %scatter_custom_fusion.1 = s32[8192]{0:T(1024)} fusion(s32[4096]{0:T(1024)S(1)} %broadcast_select_fusion.1, s32[4096]{0:T(1024)} %param.7, s32[]{:T(128)} %constant.14.clone.1), kind=kCustom, calls=%fused_computation.98 | custom fusion | bytes 33280
  38.1 7.4 %all-to-all-start = ((s32[32,1,256]{2,1,0:T(1,128)}), s32[32,1,256]{2,1,0:T(1,128)}, u32[]{:S(2)}, u32[]{:S(2)}) async-start(s32[32,1,256]{2,1,0:T(1,128)} %bitcast.5), calls=%async_computation | async-start | bytes 65536 | tf_op jit(solution)/shard_map/all_to_all | solution.py:48
  45.5 3.4 copy.56
  49.9 3.6 collective-permute-start.4
  58.5 2.4 copy.54
  60.9 12.9 %scatter_custom_fusion.2 = bf16[8192,64]{1,0:T(8,128)(2,1)} fusion(s32[4096]{0:T(1024)} %copy-done.17, bf16[4096,64]{1,0:T(8,128)(2,1)} %copy.54, bf16[]{:T(256)} %constant.33.clone.1), kind=kCustom, calls=%fused_computation.45 | custom fusion | bytes 1049088
  73.8 6.2 all_to_all.24
  80.6 9.4 %reduce.11 = bf16[32,16384]{1,0:T(8,128)(2,1)} reduce(bf16[32,1,16384]{2,1,0:T(2,128)(2,1)} %all_to_all.24, bf16[]{:T(256)} %broadcast.231), dimensions={1}, to_apply=%all_to_all.24.reduce_sub_computation | reduce | bytes 2097154 | tf_op jit(solution)/shard_map/all_to_all | solution.py:47
  89.9 2.6 reshape.224
  106.1 7.6 %all-to-all-start.1 = ((bf16[32,2,8192]{2,1,0:T(2,128)(2,1)}), bf16[32,2,8192]{2,1,0:T(2,128)(2,1)}, u32[]{:S(2)}, u32[]{:S(2)}) async-start(bf16[32,2,8192]{2,1,0:T(2,128)(2,1)} %reshape.224), calls=%async_computation.1 | async-start | bytes 2097152 | tf_op jit(solution)/shard_map/all_to_all | solution.py:47
  122.4 9.0 %select_maximum_fusion = bf16[64,26,10,66]{0,3,2,1:T(8,128)(2,1)S(1)} fusion(bf16[64,1,10,64]{0,3,2,1:T(8,128)(2,1)S(1)} %collective-permute-done.7, bf16[64,1,10,64]{0,3,2,1:T(8,128)(2,1)S(1)} %collective-permute-done.6, bf16[64,24,1,64]{0,3,2,1:T(8,128)(2,1)} %collective-permute-done.5, bf16[64,24,8,64]{0,3,2,1:T(8,128)(2,1)S(1)} %bitcast.265, ...), kind=kLoop, calls=%fused_computation.12 | loop fusion | flops 19768320 | bytes 4326400 | tf_op jit(solution)/shard_map/concatenate | solution.py:17
  131.4 2.4 fusion.50
  133.8 11.6 %pad_maximum_fusion.1 = bf16[192,26,10,64]{0,3,2,1:T(8,128)(2,1)S(1)} fusion(bf16[64,26,10,64]{0,3,2,1:T(8,128)(2,1)S(1)} %get-tuple-element.15, bf16[64,1,10,64]{0,3,2,1:T(8,128)(2,1)S(1)} %collective-permute-done.7, bf16[64,24,1,64]{0,3,2,1:T(8,128)(2,1)} %collective-permute-done.5, bf16[64,24,8,64]{0,3,2,1:T(8,128)(2,1)S(1)} %bitcast.266, ...), kind=kLoop, calls=%fused_computation.9 | loop fusion | flops 44728320 | bytes 12779520 | tf_op jit(solution)/shard_map/concatenate | solution.py:29
  145.4 4.4 fusion.55
  149.8 4.4 fusion.56
  154.3 4.4 fusion.57
  158.7 4.4 fusion.58
  163.0 4.5 fusion.59
  167.5 4.4 fusion.60
  171.9 4.4 fusion.61
  176.3 4.9 fusion.62
  181.2 18.4 %add_convert_fusion = bf16[24,8,64,64]{3,2,1,0:T(8,128)(2,1)} fusion(f32[24,8,64,64]{3,2,1,0:T(8,128)} %fusion.62, f32[24,8,64,64]{3,2,1,0:T(8,128)} %fusion.61, f32[24,8,64,64]{3,2,1,0:T(8,128)} %fusion.60, f32[24,8,64,64]{3,2,1,0:T(8,128)} %fusion.59, f32[24,8,64,64]{3,2,1,0:T(8,128)} %fusion.58, f32[24,8,64,64]{3,2,1,0:T(8,128)} %fusion.57, ...), kind=kOutput, calls=%fused_computation.10 | convolution fusion | flops 309067776 | bytes 33153024 | tf_op jit(solution)/shard_map/ck,kxyz->cxyz/dot_general | solution.py:75
  199.6 30.4 %gather_fusion = bf16[8192,64]{1,0:T(8,128)(2,1)} fusion(bf16[64,12288]{0,1:T(8,128)(2,1)} %bitcast.281, s32[8192]{0:T(1024)S(1)} %copy-done.15), kind=kCustom, calls=%fused_computation | custom fusion | bytes 2129920 | tf_op jit(solution)/shard_map/jit(_take)/gather | solution.py:87
  230.1 6.6 broadcast_select_fusion
  236.6 6.2 all_to_all.25
  242.8 9.4 %reduce.12 = bf16[32,16384]{1,0:T(8,128)(2,1)} reduce(bf16[32,1,16384]{2,1,0:T(2,128)(2,1)} %all_to_all.25, bf16[]{:T(256)} %broadcast.231), dimensions={1}, to_apply=%all_to_all.25.reduce_sub_computation | reduce | bytes 2097154 | tf_op jit(solution)/shard_map/all_to_all | solution.py:88
  252.2 2.6 reshape.226
  254.8 21.9 %all-to-all-start.2 = ((bf16[32,2,8192]{2,1,0:T(2,128)(2,1)}), bf16[32,2,8192]{2,1,0:T(2,128)(2,1)}, u32[]{:S(2)}, u32[]{:S(2)}) async-start(bf16[32,2,8192]{2,1,0:T(2,128)(2,1)} %reshape.226), calls=%async_computation.2 | async-start | bytes 2097152 | tf_op jit(solution)/shard_map/all_to_all | solution.py:88
  276.8 5.9 reshape.225
  282.7 9.0 %convert_reduce_fusion = f32[32,16384]{1,0:T(8,128)} fusion(bf16[32,1,16384]{2,1,0:T(2,128)(2,1)} %reshape.225), kind=kLoop, calls=%fused_computation.25 | loop fusion | flops 524288 | bytes 3145728 | tf_op jit(solution)/shard_map/convert_element_type | solution.py:50
  291.7 4.3 reshape.171
  296.0 52.3 %scatter_custom_fusion = f32[12288,64]{1,0:T(8,128)} fusion(s32[8192]{0:T(1024)} %bitcast.6, f32[8192,64]{1,0:T(8,128)} %reshape.171, f32[]{:T(128)} %constant.13.clone.1), kind=kCustom, calls=%fused_computation.23 | custom fusion | flops 524288 | bytes 3146240 | tf_op jit(solution)/shard_map/scatter-add | solution.py:52
  348.3 3.0 convert_element_type.29
  351.4 8.3 %collective-permute-start = (bf16[64,24,1,64]{0,3,2,1:T(8,128)(2,1)S(1)}, bf16[64,24,1,64]{0,3,2,1:T(8,128)(2,1)S(1)}, u32[]{:S(2)}, u32[]{:S(2)}) collective-permute-start(bf16[64,24,1,64]{0,3,2,1:T(8,128)(2,1)S(1)} %get-tuple-element.24), channel_id=1, source_target_pairs={{0,8},{8,16},{16,24},{1,9},{9,17},{17,25},{2,10},{10,18},{18,26},{... | collective-permute-start | bytes 589832 | tf_op jit(solution)/shard_map/ppermute | solution.py:19
  361.1 4.0 collective-permute-done
  365.0 5.9 collective-permute-done.1
  375.1 6.2 reshape.227
  381.3 8.7 %reduce.6 = bf16[32,16384]{1,0:T(8,128)(2,1)} reduce(bf16[32,1,16384]{2,1,0:T(2,128)(2,1)} %reshape.227, bf16[]{:T(256)} %constant.72), dimensions={1}, to_apply=%all_to_all.23.reduce_sub_computation | reduce | bytes 2097154 | tf_op jit(solution)/shard_map/all_to_all | solution.py:88
  390.0 4.0 reshape.141
  394.0 67.6 %gather_fusion.1 = bf16[4096,64]{1,0:T(8,128)(2,1)} fusion(bf16[32,256,64]{2,1,0:T(8,128)(2,1)} %reshape.141, s32[4096]{0:T(1024)S(1)} %bitcast.276), kind=kCustom, calls=%fused_computation.1 | custom fusion | bytes 1081344 | tf_op jit(solution)/shard_map/gather | solution.py:90
  461.6 2.3 copy.87
  464.0 9.6 %select_maximum_fusion.4 = bf16[64,26,10,66]{0,3,2,1:T(8,128)(2,1)S(1)} fusion(bf16[64,1,10,64]{0,3,2,1:T(8,128)(2,1)} %collective-permute-done.3, bf16[64,1,10,64]{0,3,2,1:T(8,128)(2,1)} %collective-permute-done.2, bf16[64,24,1,64]{0,3,2,1:T(8,128)(2,1)} %copy-done.3, bf16[64,24,8,64]{0,3,2,1:T(8,128)(2,1)} %bitcast.279, ...), kind=kLoop, calls=%fused_computation.16 | loop fusion | flops 19768320 | bytes 4326400 | tf_op jit(solution)/shard_map/concatenate | solution.py:17
  473.6 2.3 fusion.51
  475.9 11.3 %pad_maximum_fusion = bf16[192,26,10,64]{0,3,2,1:T(8,128)(2,1)S(1)} fusion(bf16[64,26,10,64]{0,3,2,1:T(8,128)(2,1)S(1)} %get-tuple-element.17, bf16[64,1,10,64]{0,3,2,1:T(8,128)(2,1)} %collective-permute-done.3, bf16[64,24,1,64]{0,3,2,1:T(8,128)(2,1)S(1)} %copy-done.4, bf16[64,24,8,64]{0,3,2,1:T(8,128)(2,1)S(1)} %bitcast.280, ...), kind=kLoop, calls=%fused_computation.8 | loop fusion | flops 44728320 | bytes 12779520 | tf_op jit(solution)/shard_map/concatenate | solution.py:29
  487.2 2.8 fusion.16
  490.0 4.5 fusion.23
  494.4 4.3 fusion.25
  498.8 4.4 fusion.27
  503.2 4.4 fusion.29
  507.6 4.4 fusion.31
  512.0 4.3 fusion.33
  516.3 4.4 fusion.35
  520.7 2.1 fusion.15
  522.8 2.3 fusion.14
  527.3 2.1 fusion.12
  529.4 2.1 fusion.11
  533.7 2.1 fusion.9
  535.8 2.1 fusion.8
  538.0 7.2 %fusion.37 = f32[24,8,64,64]{3,2,1,0:T(8,128)} fusion(bf16[192,26,10,64]{0,3,2,1:T(8,128)(2,1)} %copy-done, bf16[9,64,192]{2,1,0:T(8,128)(2,1)S(1)} %copy-done.5), kind=kOutput, calls=%fused_computation.83 | convolution fusion | flops 301989888 | bytes 9568256 | tf_op jit(solution)/shard_map/ok,kxyz->oxyz/dot_general | solution.py:69
  545.2 58.3 %all-reduce.5.cloned.1.call-done = f32[9,64,192]{2,1,0:T(8,128)} async-done(((f32[9,64,192]{2,1,0:T(8,128)}), f32[9,64,192]{2,1,0:T(8,128)}) %all-reduce.5.cloned.1.call-update) | async-done | bytes 442384 | tf_op jit(solution)/shard_map/psum | solution.py:83
  603.5 18.7 %add_convert_fusion.1 = bf16[24,8,64,64]{3,2,1,0:T(8,128)(2,1)S(1)} fusion(f32[24,8,64,64]{3,2,1,0:T(8,128)} %fusion.23, f32[24,8,64,64]{3,2,1,0:T(8,128)} %fusion.25, f32[24,8,64,64]{3,2,1,0:T(8,128)} %fusion.27, f32[24,8,64,64]{3,2,1,0:T(8,128)} %fusion.29, f32[24,8,64,64]{3,2,1,0:T(8,128)} %fusion.31, f32[24,8,64,64]{3,2,1,0:T(8,128)} %fusion.33, ...), kind=kOutput, calls=%fused_computation.11 | convolution fusion | flops 309067776 | bytes 33161216 | tf_op jit(solution)/shard_map/ok,kxyz->oxyz/dot_general | solution.py:69
  622.3 3.1 copy.86
  625.4 26.2 %all-reduce.7.cloned.1.call-done = f32[9,64,192]{2,1,0:T(8,128)} async-done(((f32[9,64,192]{2,1,0:T(8,128)}), f32[9,64,192]{2,1,0:T(8,128)}) %all-reduce.7.cloned.1.call-update) | async-done | bytes 442384 | tf_op jit(solution)/shard_map/psum | solution.py:83
  (87 shorter events, 46.0 us)
Async XLA Ops:
  21.8 16.3 %copy-start.17 = (s32[4096]{0:T(1024)}, s32[4096]{0:T(1024)S(1)}, u32[]{:S(2)}) copy-start(s32[4096]{0:T(1024)S(1)} %broadcast_select_fusion.1) | copy-start | bytes 49156
  38.1 68.0 %all-to-all-start = ((s32[32,1,256]{2,1,0:T(1,128)}), s32[32,1,256]{2,1,0:T(1,128)}, u32[]{:S(2)}, u32[]{:S(2)}) async-start(s32[32,1,256]{2,1,0:T(1,128)} %bitcast.5), calls=%async_computation | async-start | bytes 65536 | tf_op jit(solution)/shard_map/all_to_all | solution.py:48
  49.9 65.2 %collective-permute-start.4 = (bf16[64,24,1,64]{0,3,2,1:T(8,128)(2,1)}, bf16[64,24,1,64]{0,3,2,1:T(8,128)(2,1)S(1)}, u32[]{:S(2)}, u32[]{:S(2)}) collective-permute-start(bf16[64,24,1,64]{0,3,2,1:T(8,128)(2,1)} %get-tuple-element.22), channel_id=1, source_target_pairs={{0,8},{8,16},{16,24},{1,9},{9,17},{17,25},{2,10},{10,18},{18,26},{... | collective-permute-start | bytes 589832 | tf_op jit(solution)/shard_map/ppermute | solution.py:19
  53.5 61.6 %collective-permute-start.5 = (bf16[64,24,1,64]{0,3,2,1:T(8,128)(2,1)}, bf16[64,24,1,64]{0,3,2,1:T(8,128)(2,1)}, u32[]{:S(2)}, u32[]{:S(2)}) collective-permute-start(bf16[64,24,1,64]{0,3,2,1:T(8,128)(2,1)} %get-tuple-element.23), channel_id=1, source_target_pairs={{8,0},{16,8},{24,16},{9,1},{17,9},{25,17},{10,2},{18,10},{26,18},{... | collective-permute-start | bytes 589832 | tf_op jit(solution)/shard_map/ppermute | solution.py:21
  106.1 148.8 %all-to-all-start.1 = ((bf16[32,2,8192]{2,1,0:T(2,128)(2,1)}), bf16[32,2,8192]{2,1,0:T(2,128)(2,1)}, u32[]{:S(2)}, u32[]{:S(2)}) async-start(bf16[32,2,8192]{2,1,0:T(2,128)(2,1)} %reshape.224), calls=%async_computation.1 | async-start | bytes 2097152 | tf_op jit(solution)/shard_map/all_to_all | solution.py:47
  115.9 4.8 collective-permute-start.6
  118.0 4.4 collective-permute-start.7
  133.7 11.6 %copy-start.7 = (bf16[1,64,3,64]{1,3,2,0:T(8,128)(2,1)S(1)}, bf16[1,64,3,64]{1,3,2,0:T(8,128)(2,1)}, u32[]{:S(2)}) copy-start(bf16[1,64,3,64]{1,3,2,0:T(8,128)(2,1)} %copy.58) | copy-start | bytes 73732
  145.4 4.5 copy-start.8
  149.8 4.4 copy-start.9
  154.3 4.4 copy-start.10
  158.6 4.4 copy-start.11
  163.0 4.5 copy-start.12
  167.5 4.4 copy-start.13
  171.9 4.4 copy-start.14
  176.3 4.9 copy-start.6
  181.2 18.4 %copy-start.15 = (s32[8192]{0:T(1024)S(1)}, s32[8192]{0:T(1024)}, u32[]{:S(2)}) copy-start(s32[8192]{0:T(1024)} %broadcast_clamp_fusion) | copy-start | bytes 98308
  199.6 30.4 %copy-start.16 = (pred[8192]{0:T(1024)(128)(4,1)S(1)}, pred[8192]{0:T(1024)(128)(4,1)}, u32[]{:S(2)}) copy-start(pred[8192]{0:T(1024)(128)(4,1)} %compare_and_fusion) | copy-start | bytes 24580
  254.8 120.2 %all-to-all-start.2 = ((bf16[32,2,8192]{2,1,0:T(2,128)(2,1)}), bf16[32,2,8192]{2,1,0:T(2,128)(2,1)}, u32[]{:S(2)}, u32[]{:S(2)}) async-start(bf16[32,2,8192]{2,1,0:T(2,128)(2,1)} %reshape.226), calls=%async_computation.2 | async-start | bytes 2097152 | tf_op jit(solution)/shard_map/all_to_all | solution.py:88
  276.8 326.7 %all-reduce.5.cloned.1.call-start = ((), (), s32[]{:S(2)}) async-start(), calls=%async_computation.3 | async-start | bytes 1179648 | tf_op jit(solution)/shard_map/psum | solution.py:83
  351.4 19.6 %copy-start.1 = (bf16[12288,64]{1,0:T(8,128)(2,1)}, bf16[12288,64]{1,0:T(8,128)(2,1)S(1)}, u32[]{:S(2)}) copy-start(bf16[12288,64]{1,0:T(8,128)(2,1)S(1)} %convert_element_type.29) | copy-start | bytes 4718596
  351.4 13.6 %collective-permute-start = (bf16[64,24,1,64]{0,3,2,1:T(8,128)(2,1)S(1)}, bf16[64,24,1,64]{0,3,2,1:T(8,128)(2,1)S(1)}, u32[]{:S(2)}, u32[]{:S(2)}) collective-permute-start(bf16[64,24,1,64]{0,3,2,1:T(8,128)(2,1)S(1)} %get-tuple-element.24), channel_id=1, source_target_pairs={{0,8},{8,16},{16,24},{1,9},{9,17},{17,25},{2,10},{10,18},{18,26},{... | collective-permute-start | bytes 589832 | tf_op jit(solution)/shard_map/ppermute | solution.py:19
  359.8 11.2 %collective-permute-start.1 = (bf16[64,24,1,64]{0,3,2,1:T(8,128)(2,1)S(1)}, bf16[64,24,1,64]{0,3,2,1:T(8,128)(2,1)S(1)}, u32[]{:S(2)}, u32[]{:S(2)}) collective-permute-start(bf16[64,24,1,64]{0,3,2,1:T(8,128)(2,1)S(1)} %get-tuple-element.25), channel_id=1, source_target_pairs={{8,0},{16,8},{24,16},{9,1},{17,9},{25,17},{10,2},{18,10},{26,18},{... | collective-permute-start | bytes 589832 | tf_op jit(solution)/shard_map/ppermute | solution.py:21
  370.9 0.9 copy-start.3
  371.8 92.2 %collective-permute-start.2 = (bf16[64,1,10,64]{0,3,2,1:T(8,128)(2,1)}, bf16[64,1,10,64]{0,3,2,1:T(8,128)(2,1)}, u32[]{:S(2)}, u32[]{:S(2)}) collective-permute-start(bf16[64,1,10,64]{0,3,2,1:T(8,128)(2,1)} %get-tuple-element.20), channel_id=1, source_target_pairs={{0,1},{1,2},{2,3},{3,4},{4,5},{5,6},{6,7},{8,9},{9,10},{10,11},{11... | collective-permute-start | bytes 245768 | tf_op jit(solution)/shard_map/ppermute | solution.py:19
  373.8 90.2 %collective-permute-start.3 = (bf16[64,1,10,64]{0,3,2,1:T(8,128)(2,1)}, bf16[64,1,10,64]{0,3,2,1:T(8,128)(2,1)}, u32[]{:S(2)}, u32[]{:S(2)}) collective-permute-start(bf16[64,1,10,64]{0,3,2,1:T(8,128)(2,1)} %get-tuple-element.21), channel_id=1, source_target_pairs={{1,0},{2,1},{3,2},{4,3},{5,4},{6,5},{7,6},{9,8},{10,9},{11,10},{12... | collective-permute-start | bytes 245768 | tf_op jit(solution)/shard_map/ppermute | solution.py:21
  473.5 2.4 copy-start.2
  473.6 2.4 copy-start.4
  487.2 48.6 %copy-start = (bf16[192,26,10,64]{0,3,2,1:T(8,128)(2,1)}, bf16[192,26,10,64]{0,3,2,1:T(8,128)(2,1)S(1)}, u32[]{:S(2)}) copy-start(bf16[192,26,10,64]{0,3,2,1:T(8,128)(2,1)S(1)} %pad_maximum_fusion) | copy-start | bytes 19169284
  487.2 2.8 copy-start.5
  538.0 113.7 %all-reduce.7.cloned.1.call-start = ((), (), s32[]{:S(2)}) async-start(), calls=%async_computation.4 | async-start | bytes 1179648 | tf_op jit(solution)/shard_map/psum | solution.py:83
Sparse Core Ops, SparseCore 0:
  538.1 65.3 all-reduce.4
  606.5 45.0 all-reduce.6
